TPU v7x, 32 devices: a whole 2x2x4 slice. The times are simulated.
32 devices in a mesh: seg: 4 (over z), mem: 8 (over y, x, core).
Axes of the slice: x: 2, y: 2, z: 4, core: 2. Of those that a mesh axis runs over, the one named last changes fastest.
Arguments:
- tokens: bfloat16 [8192, 1024], P(('seg', 'mem')), may hold values from -6 to 6
- padding_mask: int32 [8192], P(('seg', 'mem')), may hold values from 0 to 1, as said below
- memory_keys: bfloat16 [4, 8192, 1024], P('seg', 'mem'), may hold values from -6 to 6
- memory_values: bfloat16 [4, 8192, 1024], P('seg', 'mem'), may hold values from -6 to 6
- memory_length: int32 [4], P('seg'), may hold values from 2048 to 8192, as said below
- chosen_keys: int32 [16, 128], P('seg'), may hold values from 0 to 8191, as said below
- norm_gain: float32 [1024], replicated, may hold values from 0.1 to 1.9
- w_query: bfloat16 [1024, 1024], replicated, may hold values from -0.1875 to 0.1875
- w_key: bfloat16 [1024, 1024], replicated, may hold values from -0.1875 to 0.1875
- w_value: bfloat16 [1024, 1024], replicated, may hold values from -0.1875 to 0.1875
- w_out: bfloat16 [1024, 1024], replicated, may hold values from -1.5 to 1.5
- ffn_gain: float32 [1024], replicated, may hold values from 0.1 to 1.9
- w_gate: bfloat16 [1024, 2816], replicated, may hold values from -0.1875 to 0.1875
- w_up: bfloat16 [1024, 2816], replicated, may hold values from -0.1875 to 0.1875
- w_down: bfloat16 [2816, 1024], replicated, may hold values from -0.109375 to 0.109375
- cotangent: bfloat16 [8192, 1024], P(('seg', 'mem')), may hold values from -6 to 6
Outputs:
- mixed: bfloat16 [8192, 1024], P(('seg', 'mem'))
- input_grad: bfloat16 [8192, 1024], P(('seg', 'mem'))
- norm_gain_grad: float32 [1024], P('mem')
- query_grad: float32 [1024, 1024], P('mem')
- key_grad: float32 [1024, 1024], P('mem')
- value_grad: float32 [1024, 1024], P('mem')
- out_grad: float32 [1024, 1024], P('mem')
- ffn_gain_grad: float32 [1024], P('mem')
- gate_grad: float32 [1024, 2816], P('mem')
- up_grad: float32 [1024, 2816], P('mem')
- down_grad: float32 [2816, 1024], P('mem')
Inputs may be any that keep to these rules, and one draw needn't show every extreme that they name: `padding_mask`: within each segment of 2048 consecutive tokens the ones form a prefix of 1024 tokens or more. `memory_length`: how many of a segment's 8192 memory slots are live. `chosen_keys`: row b belongs to the queries b * 512 to (b + 1) * 512 - 1; its first entry is below 2048.
All inputs are finite; a program needn't handle non-finite values.
Results may differ from a plain program's by a relative error of at most 0.014.
Values may be sent and summed in bfloat16 or wider, within the bound.
No kernel may reach another device: no remote copies, remote signals or barrier semaphores. Data moves between devices by JAX's collectives and lax.ppermute only.
A program may use at most 320 MiB of HBM per device.

v0:
```python
import math
import jax
import jax.numpy as jnp
from jax import lax
from jax.sharding import PartitionSpec as P

H = 8
HD = 128
SEG_LEN = 2048
QB = 512
TOPK = 128
EPSILON = 1e-05
NEGATIVE = -1e30


def outer_product(left, right):
    return lax.dot_general(
        left, right, (((0,), (0,)), ((), ())), preferred_element_type=jnp.float32
    )


def backward_dot(left, weight):
    return lax.dot_general(
        left, weight, (((1,), (1,)), ((), ())), preferred_element_type=jnp.float32
    )


def forward_dot(left, weight):
    return jnp.dot(left, weight, preferred_element_type=jnp.float32)


def normalize(values):
    factor = lax.rsqrt(jnp.mean(values * values, axis=-1, keepdims=True) + EPSILON)
    return (values * factor, factor)


def norm_back(grad_in, normed, factor, gain):
    scaled = grad_in * gain
    return factor * (scaled - normed * jnp.mean(scaled * normed, axis=-1, keepdims=True))


def block_stats(scores, usable):
    highest = jnp.max(scores, axis=-1)
    row_sum = jnp.sum(jnp.where(usable, jnp.exp(scores - highest[..., None]), 0.0), axis=-1)
    return (highest, row_sum)


def join_stats(high_left, sum_left, high_right, sum_right):
    highest = jnp.maximum(high_left, high_right)
    return (
        highest,
        sum_left * jnp.exp(high_left - highest) + sum_right * jnp.exp(high_right - highest),
    )


def local(
    tokens,
    padding_mask,
    memory_keys,
    memory_values,
    memory_length,
    chosen_keys,
    norm_gain,
    w_query,
    w_key,
    w_value,
    w_out,
    ffn_gain,
    w_gate,
    w_up,
    w_down,
    cotangent,
):
    group_size = lax.axis_size("mem")
    position = lax.axis_index("mem")
    tok_rows, model_width = tokens.shape
    memory_rows = memory_keys.shape[1]
    segment_count = memory_keys.shape[0]
    all_rows = tok_rows * group_size
    blocks = all_rows // QB
    segment_blocks = SEG_LEN // QB
    score_scale = 1.0 / math.sqrt(HD)
    inputs = tokens.astype(jnp.float32)
    normed_one, factor_one = normalize(inputs)
    h_one = (normed_one * norm_gain).astype(jnp.bfloat16)
    queries = forward_dot(h_one, w_query).astype(jnp.bfloat16)
    keyed_flat = forward_dot(h_one, w_key).astype(jnp.bfloat16)
    valued_flat = forward_dot(h_one, w_value).astype(jnp.bfloat16)
    own_keys = keyed_flat.reshape(tok_rows, H, HD)
    own_values = valued_flat.reshape(tok_rows, H, HD)
    first_row = position * tok_rows
    own_segment = first_row // SEG_LEN
    own_offset = first_row % SEG_LEN
    start_block = own_segment * segment_blocks
    key_position = own_offset + jnp.arange(tok_rows)
    key_usable = padding_mask == 1
    block_segment = jnp.arange(blocks) * QB // SEG_LEN
    segment_match = block_segment[:, None] == jnp.arange(segment_count)[None, :]
    limits = jnp.sum(jnp.where(segment_match, memory_length[None, :], 0), axis=1)
    shifted = chosen_keys - position * memory_rows
    owned = (shifted >= 0) & (shifted < memory_rows) & (chosen_keys < limits[:, None])
    columns = jnp.arange(memory_rows)

    def select_slots(pieces):
        local_rows, usable, segment = pieces
        table = ((local_rows[:, None] == columns[None, :]) & usable[:, None]).astype(jnp.bfloat16)
        keys_here = lax.dynamic_index_in_dim(memory_keys, segment, 0, keepdims=False)
        values_here = lax.dynamic_index_in_dim(memory_values, segment, 0, keepdims=False)
        return (
            forward_dot(table, keys_here).astype(jnp.bfloat16),
            forward_dot(table, values_here).astype(jnp.bfloat16),
        )

    picked_keys, picked_values = lax.map(select_slots, (shifted, owned, block_segment))
    gathered = lax.all_gather(queries, "mem", axis=0, tiled=True).reshape(blocks, QB, H, HD)
    picked_keys = picked_keys.reshape(blocks, TOPK, H, HD)
    picked_values = picked_values.reshape(blocks, TOPK, H, HD)

    def memory_scores(query_block, key_block, usable):
        scores = (
            jnp.einsum("qhd,thd->qht", query_block, key_block, preferred_element_type=jnp.float32)
            * score_scale
        )
        return jnp.where(usable[None, None, :], scores, NEGATIVE)

    def local_visible(block_index):
        query_position = block_index * QB + jnp.arange(QB)
        return (key_position[None, :] <= query_position[:, None]) & key_usable[None, :]

    def local_scores(query_block, visible):
        scores = (
            jnp.einsum("qhd,khd->qhk", query_block, own_keys, preferred_element_type=jnp.float32)
            * score_scale
        )
        return jnp.where(visible[:, None, :], scores, NEGATIVE)

    def segment_rows(source, block_index):
        return lax.dynamic_index_in_dim(source, start_block + block_index, 0, keepdims=False)

    def add_segment(whole, local_part):
        merged = lax.dynamic_slice_in_dim(whole, start_block, segment_blocks, 0) + local_part
        return lax.dynamic_update_slice_in_dim(whole, merged, start_block, 0)

    def memory_first(pieces):
        query_block, key_block, usable = pieces
        return block_stats(memory_scores(query_block, key_block, usable), usable[None, None, :])

    memory_high, memory_sum = lax.map(memory_first, (gathered, picked_keys, owned))

    def local_first(block_index):
        visible = local_visible(block_index)
        scores = local_scores(segment_rows(gathered, block_index), visible)
        return block_stats(scores, visible[:, None, :])

    local_high, local_sum = lax.map(local_first, jnp.arange(segment_blocks))
    seg_high = lax.dynamic_slice_in_dim(memory_high, start_block, segment_blocks, 0)
    seg_sum = lax.dynamic_slice_in_dim(memory_sum, start_block, segment_blocks, 0)
    seg_high, seg_sum = join_stats(seg_high, seg_sum, local_high, local_sum)
    memory_high = lax.dynamic_update_slice_in_dim(memory_high, seg_high, start_block, 0)
    memory_sum = lax.dynamic_update_slice_in_dim(memory_sum, seg_sum, start_block, 0)
    row_high = lax.pmax(memory_high.astype(jnp.bfloat16), "mem").astype(memory_high.dtype)
    row_sum = lax.psum(memory_sum * jnp.exp(memory_high - row_high), "mem")
    log_total = row_high + jnp.log(row_sum)

    def memory_second(pieces):
        query_block, key_block, value_block, usable, block_total = pieces
        scores = memory_scores(query_block, key_block, usable)
        weights = jnp.where(
            usable[None, None, :], jnp.exp(scores - block_total[..., None]), 0.0
        ).astype(jnp.bfloat16)
        return jnp.einsum("qht,thd->qhd", weights, value_block, preferred_element_type=jnp.float32)

    numerators = lax.map(memory_second, (gathered, picked_keys, picked_values, owned, log_total))

    def local_second(block_index):
        visible = local_visible(block_index)
        scores = local_scores(segment_rows(gathered, block_index), visible)
        block_total = segment_rows(log_total, block_index)
        weights = jnp.where(
            visible[:, None, :], jnp.exp(scores - block_total[..., None]), 0.0
        ).astype(jnp.bfloat16)
        return jnp.einsum("qhk,khd->qhd", weights, own_values, preferred_element_type=jnp.float32)

    numerators = add_segment(numerators, lax.map(local_second, jnp.arange(segment_blocks)))
    attended_sum = lax.psum_scatter(
        numerators.reshape(all_rows, model_width), "mem", scatter_dimension=0, tiled=True
    )
    attended = attended_sum.astype(jnp.bfloat16)
    residual = inputs + forward_dot(attended, w_out)
    normed_two, factor_two = normalize(residual)
    h_two = (normed_two * ffn_gain).astype(jnp.bfloat16)
    gate = forward_dot(h_two, w_gate)
    up_part = forward_dot(h_two, w_up)
    sigmoid_gate = jax.nn.sigmoid(gate)
    silu_gate = gate * sigmoid_gate
    act = (silu_gate * up_part).astype(jnp.bfloat16)
    mixed = (residual + forward_dot(act, w_down)).astype(jnp.bfloat16)
    down_grad = outer_product(act, cotangent)
    d_act = backward_dot(cotangent, w_down)
    d_gate = (d_act * up_part * sigmoid_gate * (1.0 + gate * (1.0 - sigmoid_gate))).astype(
        jnp.bfloat16
    )
    d_up = (d_act * silu_gate).astype(jnp.bfloat16)
    gate_grad = outer_product(h_two, d_gate)
    up_grad = outer_product(h_two, d_up)
    d_two = backward_dot(d_gate, w_gate) + backward_dot(d_up, w_up)
    ffn_gain_grad = jnp.sum(d_two * normed_two, axis=0)
    d_res = cotangent.astype(jnp.float32) + norm_back(d_two, normed_two, factor_two, ffn_gain)
    d_res_low = d_res.astype(jnp.bfloat16)
    out_grad = outer_product(attended, d_res_low)
    d_att = backward_dot(d_res_low, w_out).astype(jnp.bfloat16)
    grad_rows = lax.all_gather(d_att, "mem", axis=0, tiled=True).reshape(blocks, QB, H, HD)

    def memory_third(pieces):
        query_block, key_block, value_block, usable, block_total, grad_block = pieces
        scores = memory_scores(query_block, key_block, usable)
        probs = jnp.where(usable[None, None, :], jnp.exp(scores - block_total[..., None]), 0.0)
        pushes = jnp.einsum(
            "qhd,thd->qht", grad_block, value_block, preferred_element_type=jnp.float32
        )
        return jnp.sum(probs * pushes, axis=-1)

    delta_part = lax.map(
        memory_third, (gathered, picked_keys, picked_values, owned, log_total, grad_rows)
    )

    def local_third(block_index):
        visible = local_visible(block_index)
        scores = local_scores(segment_rows(gathered, block_index), visible)
        block_total = segment_rows(log_total, block_index)
        probs = jnp.where(visible[:, None, :], jnp.exp(scores - block_total[..., None]), 0.0)
        pushes = jnp.einsum(
            "qhd,khd->qhk",
            segment_rows(grad_rows, block_index),
            own_values,
            preferred_element_type=jnp.float32,
        )
        return jnp.sum(probs * pushes, axis=-1)

    delta_part = add_segment(delta_part, lax.map(local_third, jnp.arange(segment_blocks)))
    delta = lax.psum(delta_part, "mem")

    def memory_fourth(pieces):
        query_block, key_block, value_block, usable, block_total, grad_block, block_delta = pieces
        scores = memory_scores(query_block, key_block, usable)
        probs = jnp.where(usable[None, None, :], jnp.exp(scores - block_total[..., None]), 0.0)
        pushes = jnp.einsum(
            "qhd,thd->qht", grad_block, value_block, preferred_element_type=jnp.float32
        )
        d_scores = jnp.where(
            usable[None, None, :], probs * (pushes - block_delta[..., None]), 0.0
        ).astype(jnp.bfloat16)
        return (
            jnp.einsum("qht,thd->qhd", d_scores, key_block, preferred_element_type=jnp.float32)
            * score_scale
        )

    query_terms = lax.map(
        memory_fourth, (gathered, picked_keys, picked_values, owned, log_total, grad_rows, delta)
    )

    def local_fourth(running, block_index):
        key_acc, value_acc = running
        visible = local_visible(block_index)
        query_block = segment_rows(gathered, block_index)
        grad_block = segment_rows(grad_rows, block_index)
        scores = local_scores(query_block, visible)
        block_total = segment_rows(log_total, block_index)
        block_delta = segment_rows(delta, block_index)
        probs = jnp.where(visible[:, None, :], jnp.exp(scores - block_total[..., None]), 0.0)
        pushes = jnp.einsum(
            "qhd,khd->qhk", grad_block, own_values, preferred_element_type=jnp.float32
        )
        d_scores = jnp.where(
            visible[:, None, :], probs * (pushes - block_delta[..., None]), 0.0
        ).astype(jnp.bfloat16)
        query_term = (
            jnp.einsum("qhk,khd->qhd", d_scores, own_keys, preferred_element_type=jnp.float32)
            * score_scale
        )
        key_acc = (
            key_acc
            + jnp.einsum("qhk,qhd->khd", d_scores, query_block, preferred_element_type=jnp.float32)
            * score_scale
        )
        value_acc = value_acc + jnp.einsum(
            "qhk,qhd->khd",
            probs.astype(jnp.bfloat16),
            grad_block,
            preferred_element_type=jnp.float32,
        )
        return ((key_acc, value_acc), query_term)

    empty_acc = jnp.zeros((tok_rows, H, HD), jnp.float32)
    (key_sum, value_sum), local_terms = lax.scan(
        local_fourth, (empty_acc, empty_acc), jnp.arange(segment_blocks)
    )
    query_terms = add_segment(query_terms, local_terms)
    d_query = lax.psum_scatter(
        query_terms.reshape(all_rows, model_width), "mem", scatter_dimension=0, tiled=True
    ).astype(jnp.bfloat16)
    d_key = key_sum.reshape(tok_rows, model_width).astype(jnp.bfloat16)
    d_value = value_sum.reshape(tok_rows, model_width).astype(jnp.bfloat16)
    query_grad = outer_product(h_one, d_query)
    key_grad = outer_product(h_one, d_key)
    value_grad = outer_product(h_one, d_value)
    d_one = (
        backward_dot(d_query, w_query) + backward_dot(d_key, w_key) + backward_dot(d_value, w_value)
    )
    norm_gain_grad = jnp.sum(d_one * normed_one, axis=0)
    input_grad = (d_res + norm_back(d_one, normed_one, factor_one, norm_gain)).astype(jnp.bfloat16)
    shards = (
        lax.psum_scatter(norm_gain_grad, "mem", scatter_dimension=0, tiled=True),
        lax.psum_scatter(query_grad, "mem", scatter_dimension=0, tiled=True),
        lax.psum_scatter(key_grad, "mem", scatter_dimension=0, tiled=True),
        lax.psum_scatter(value_grad, "mem", scatter_dimension=0, tiled=True),
        lax.psum_scatter(out_grad, "mem", scatter_dimension=0, tiled=True),
        lax.psum_scatter(ffn_gain_grad, "mem", scatter_dimension=0, tiled=True),
        lax.psum_scatter(gate_grad, "mem", scatter_dimension=0, tiled=True),
        lax.psum_scatter(up_grad, "mem", scatter_dimension=0, tiled=True),
        lax.psum_scatter(down_grad, "mem", scatter_dimension=0, tiled=True),
    )
    (
        norm_part,
        query_part,
        key_part,
        value_part,
        out_part,
        ffn_gain_part,
        gate_part,
        up_grad_part,
        down_part,
    ) = shards
    summed = lax.psum(
        (
            norm_part,
            query_part,
            key_part,
            value_part,
            out_part,
            ffn_gain_part,
            gate_part,
            up_grad_part,
            down_part,
        ),
        "seg",
    )
    (
        norm_done,
        query_done,
        key_done,
        value_done,
        out_done,
        ffn_gain_done,
        gate_done,
        up_done,
        down_done,
    ) = summed
    return (
        mixed,
        input_grad,
        norm_done,
        query_done,
        key_done,
        value_done,
        out_done,
        ffn_gain_done,
        gate_done,
        up_done,
        down_done,
    )


def solution(mesh):
    return jax.shard_map(
        local,
        mesh=mesh,
        in_specs=(
            P(("seg", "mem"), None),
            P(("seg", "mem")),
            P("seg", "mem", None),
            P("seg", "mem", None),
            P("seg"),
            P("seg", None),
            P(),
            P(),
            P(),
            P(),
            P(),
            P(),
            P(),
            P(),
            P(),
            P(("seg", "mem"), None),
        ),
        out_specs=(
            P(("seg", "mem"), None),
            P(("seg", "mem"), None),
            P("mem"),
            P("mem", None),
            P("mem", None),
            P("mem", None),
            P("mem", None),
            P("mem"),
            P("mem", None),
            P("mem", None),
            P("mem", None),
        ),
        check_vma=False,
    )
```

profile of v0, /device:TPU:0, one launch (start us, length us, event | category | flops | bytes accessed | tf_op | source)
XLA Modules:
  0.0 1458.7 jit_solution(2463133091801142676)
XLA Ops:
  15.4 22.5 %while.110 = (s32[]{:T(128)}, bf16[4,128,1024]{2,1,0:T(8,128)(2,1)}, bf16[4,128,1024]{2,1,0:T(8,128)(2,1)}, s32[4,128]{1,0:T(4,128)S(1)}, pred[4,128]{1,0:T(4,12...) while((s32[]{:T(128)}, bf16[4,128,1024]{2,1,0:T(8,128)(2,1)}, ...), condition=%wide.region_2.3_spmd.clone, body=%wide.region_1.2_spmd.clone.sunk | while | flops 537657344 | bytes 4721261 | solution.py:114
  40.4 11.2 all-gather.3.cloned.1.call-done
  57.8 20.9 %while.111 = (s32[]{:T(128)}, f32[4,512,8]{1,2,0:T(8,128)S(1)}, f32[4,512,8]{1,2,0:T(8,128)S(1)}, s32[4]{0:T(128)S(1)}, pred[256]{0:T(512)(128)(4,1)S(1)}, /*ind...) while((s32[]{:T(128)}, f32[4,512,8]{1,2,0:T(8,128)S(1)}, ...), condition=%wide.region_10.11_spmd.clone, body=%wide.region_7.10_spmd.clone.sunk | while | flops 277078784 | bytes 10475995 | solution.py:155
  78.8 9.8 while.106
  88.6 23.5 %pmax.7 = bf16[4,512,8]{1,2,0:T(8,128)(2,1)S(1)} all-reduce(bf16[4,512,8]{1,2,0:T(8,128)(2,1)S(1)} %get-tuple-element.1010), channel_id=1, replica_groups=mesh['seg'=4,'mem'=8] {'mem'}, use_global_device_ids=true, to_apply=%region_11.12 | all-reduce | flops 16384 | bytes 65536 | tf_op jit(solution)/shard_map/pmax | solution.py:161
  119.1 46.3 %all-reduce.9.cloned.1.call-done = f32[4,512,8]{1,2,0:T(8,128)} async-done(((f32[4,512,8]{1,2,0:T(8,128)}), f32[4,512,8]{1,2,0:T(8,128)}) %all-reduce.9.cloned.1.call-update) | async-done | bytes 65552 | tf_op jit(solution)/shard_map/psum | solution.py:162
  166.3 4.2 broadcast.311.clone3.1
  170.5 26.2 %while.112 = (s32[]{:T(128)}, f32[4,512,8,128]{3,1,2,0:T(8,128)}, s32[4]{0:T(128)S(1)}, pred[256]{0:T(512)(128)(4,1)S(1)}, s32[]{:T(128)}, /*index=5*/bf16[4,512...) while((s32[]{:T(128)}, f32[4,512,8,128]{3,1,2,0:T(8,128)}, ...), condition=%wide.region_16.17_spmd.clone, body=%wide.region_15.16_spmd.clone.sunk | while | flops 542376704 | bytes 4643303 | solution.py:184
  172.6 4.4 bitcast_dynamic-update-slice_fusion.17
  179.2 4.4 bitcast_dynamic-update-slice_fusion.17
  185.7 4.5 bitcast_dynamic-update-slice_fusion.17
  192.3 4.5 bitcast_dynamic-update-slice_fusion.17
  201.0 46.6 %while.107 = (s32[]{:T(128)}, f32[4,512,8,128]{3,1,2,0:T(8,128)}, bf16[4,128,8,128]{3,2,1,0:T(8,128)(2,1)}, pred[4,128]{1,0:T(4,128)(4,1)S(1)}, bf16[4,128,8,128...) while((s32[]{:T(128)}, f32[4,512,8,128]{3,1,2,0:T(8,128)}, ...), condition=%wide.region_14.15_spmd, body=%wide.region_13.14_spmd.sunk | while | flops 271056896 | bytes 13158765 | solution.py:173
  247.5 10.3 add.250
  257.8 8.2 copy.98
  266.1 5.3 copy.150
  271.5 70.8 %reduce-scatter.10.cloned.1.call-done = f32[256,1024]{1,0:T(8,128)} async-done(((f32[2048,1024]{1,0:T(8,128)}), f32[256,1024]{1,0:T(8,128)}) %reduce-scatter.10.cloned.1.call-update) | async-done | bytes 1048592 | tf_op jit(solution)/shard_map/reduce_scatter | solution.py:185
  345.4 6.3 fusion.216
  355.0 5.9 multiply_convert_fusion
  370.4 34.3 %all-gather.5.cloned.1.call-done = bf16[2048,1024]{1,0:T(8,128)(2,1)} async-done(((bf16[256,1024]{1,0:T(8,128)(2,1)}), bf16[2048,1024]{1,0:T(8,128)(2,1)}) %all-gather.5.cloned.1.call-update) | async-done | bytes 4194320 | tf_op jit(solution)/shard_map/all_gather | solution.py:212
  410.9 28.1 %while.113 = (s32[]{:T(128)}, f32[4,512,8]{1,2,0:T(8,128)S(1)}, s32[4]{0:T(128)S(1)}, pred[256]{0:T(512)(128)(4,1)S(1)}, s32[]{:T(128)}, /*index=5*/bf16[4,512,8...) while((s32[]{:T(128)}, f32[4,512,8]{1,2,0:T(8,128)S(1)}, ...), condition=%wide.region_25.26_spmd.clone, body=%wide.region_23.25_spmd.clone.sunk | while | flops 543421184 | bytes 12032499 | solution.py:240
  439.0 15.7 %while.108 = (s32[]{:T(128)}, f32[4,512,8]{1,2,0:T(8,128)S(1)}, pred[4,128]{1,0:T(4,128)(4,1)S(1)}, bf16[4,128,8,128]{3,1,2,0:T(8,128)(2,1)}, bf16[4,512,8,128]{...) while((s32[]{:T(128)}, f32[4,512,8]{1,2,0:T(8,128)S(1)}, ...), condition=%wide.region_22.23_spmd, body=%wide.region_20.22_spmd.sunk | while | flops 271577088 | bytes 6917489 | solution.py:223
  455.5 52.6 %all-reduce.11.cloned.1.call-done = f32[4,512,8]{1,2,0:T(8,128)} async-done(((f32[4,512,8]{1,2,0:T(8,128)}), f32[4,512,8]{1,2,0:T(8,128)}) %all-reduce.11.cloned.1.call-update) | async-done | bytes 65552 | tf_op jit(solution)/shard_map/psum | solution.py:241
  512.3 55.4 %while.109 = (s32[]{:T(128)}, f32[4,512,8,128]{3,1,2,0:T(8,128)}, bf16[4,128,8,128]{3,1,2,0:T(8,128)(2,1)}, pred[4,128]{1,0:T(4,128)(4,1)S(1)}, bf16[4,512,8,128...) while((s32[]{:T(128)}, f32[4,512,8,128]{3,1,2,0:T(8,128)}, ...), condition=%wide.region_28.29_spmd, body=%wide.region_27.28_spmd.sunk | while | flops 407371776 | bytes 17665912 | solution.py:258
  515.6 4.6 multiply_bitcast_fusion.2
  529.4 4.6 multiply_bitcast_fusion.2
  543.3 4.6 multiply_bitcast_fusion.2
  557.0 4.6 multiply_bitcast_fusion.2
  571.9 50.7 %while.114 = (s32[]{:T(128)}, f32[256,8,128]{0,2,1:T(8,128)}, f32[256,8,128]{0,2,1:T(8,128)}, f32[4,512,8,128]{3,1,2,0:T(8,128)}, s32[4]{0:T(128)S(1)}, /*index=...) while((s32[]{:T(128)}, f32[256,8,128]{0,2,1:T(8,128)}, ...), condition=%wide.region_30.31_spmd.clone, body=%wide.region_29.30_spmd.clone.sunk | while | flops 1357906688 | bytes 65264296 | solution.py:295
  622.6 10.3 add.259
  632.9 8.2 copy.117
  641.1 5.4 copy.149
  646.6 4.4 fusion.199
  661.5 7.7 fusion.219
  669.2 7.4 fusion.218
  676.7 7.6 fusion.220
  684.4 33.0 %reduce-scatter.12.cloned.1.call-done = f32[256,1024]{1,0:T(8,128)} async-done(((f32[2048,1024]{1,0:T(8,128)}), f32[256,1024]{1,0:T(8,128)}) %reduce-scatter.12.cloned.1.call-update) | async-done | bytes 1048592 | tf_op jit(solution)/shard_map/reduce_scatter | solution.py:299
  721.5 50.6 %reduce-scatter.20.cloned.1.call-done = f32[128,1024]{1,0:T(8,128)} async-done(((f32[1024,1024]{1,0:T(8,128)}), f32[128,1024]{1,0:T(8,128)}) %reduce-scatter.20.cloned.1.call-update) | async-done | bytes 524304 | tf_op jit(solution)/shard_map/reduce_scatter | solution.py:317
  772.1 55.1 %reduce-scatter.18.cloned.1.call-done = f32[128,1024]{1,0:T(8,128)} async-done(((f32[1024,1024]{1,0:T(8,128)}), f32[128,1024]{1,0:T(8,128)}) %reduce-scatter.18.cloned.1.call-update) | async-done | bytes 524304 | tf_op jit(solution)/shard_map/reduce_scatter | solution.py:316
  827.2 54.7 %reduce-scatter.16.cloned.1.call-done = f32[128,1024]{1,0:T(8,128)} async-done(((f32[1024,1024]{1,0:T(8,128)}), f32[128,1024]{1,0:T(8,128)}) %reduce-scatter.16.cloned.1.call-update) | async-done | bytes 524304 | tf_op jit(solution)/shard_map/reduce_scatter | solution.py:315
  881.9 90.6 %reduce-scatter.24.cloned.1.call-done = f32[128,2816]{1,0:T(8,128)} async-done(((f32[1024,2816]{1,0:T(8,128)}), f32[128,2816]{1,0:T(8,128)}) %reduce-scatter.24.cloned.1.call-update) | async-done | bytes 1441808 | tf_op jit(solution)/shard_map/reduce_scatter | solution.py:320
  972.4 90.7 %reduce-scatter.22.cloned.1.call-done = f32[128,2816]{1,0:T(8,128)} async-done(((f32[1024,2816]{1,0:T(8,128)}), f32[128,2816]{1,0:T(8,128)}) %reduce-scatter.22.cloned.1.call-update) | async-done | bytes 1441808 | tf_op jit(solution)/shard_map/reduce_scatter | solution.py:319
  1063.1 90.5 %reduce-scatter.26.cloned.1.call-done = f32[352,1024]{1,0:T(8,128)} async-done(((f32[2816,1024]{1,0:T(8,128)}), f32[352,1024]{1,0:T(8,128)}) %reduce-scatter.26.cloned.1.call-update) | async-done | bytes 1441808 | tf_op jit(solution)/shard_map/reduce_scatter | solution.py:321
  1153.7 55.0 %reduce-scatter.14.cloned.1.call-done = f32[128,1024]{1,0:T(8,128)} async-done(((f32[1024,1024]{1,0:T(8,128)}), f32[128,1024]{1,0:T(8,128)}) %reduce-scatter.14.cloned.1.call-update) | async-done | bytes 524304 | tf_op jit(solution)/shard_map/reduce_scatter | solution.py:314
  1210.0 5.9 fusion.184
  1221.0 13.1 all-reduce.2
  1234.3 12.5 all-reduce.3
  1249.5 191.5 %all-reduce.13.cloned.1.call-done = (f32[128,1024]{1,0:T(8,128)}, f32[128,1024]{1,0:T(8,128)}, f32[128,1024]{1,0:T(8,128)}, f32[128,1024]{1,0:T(8,128)}, f32[128...) async-done(((f32[128,1024]{1,0:T(8,128)}, f32[128,1024]{1,0:T(8,128)}, f32[128,1024]{1,0:T(8,128)}, f32[128,1024]{1,0:T(8,128)}, f32[128,2816]{1,0:T(8,128)}, ...) | async-done | bytes 6422544 | tf_op jit(solution)/shard_map/psum | solution.py:334
  (429 shorter events, 309.7 us)
Async XLA Ops:
  7.2 106.0 %copy-start = (bf16[1024,1024]{1,0:T(8,128)(2,1)S(1)}, bf16[1024,1024]{1,0:T(8,128)(2,1)}, u32[]{:S(2)}) copy-start(bf16[1024,1024]{1,0:T(8,128)(2,1)} %param.43) | copy-start | bytes 6291460
  7.2 5.6 copy-start.3
  7.2 5.6 copy-start.25
  7.2 44.4 %all-gather.3.cloned.1.call-start = ((), (), s32[]{:S(2)}) async-start(), calls=%async_computation.9 | async-start | bytes 4718592 | tf_op jit(solution)/shard_map/all_gather | solution.py:115
  8.6 104.5 %copy-start.27 = (f32[256]{0:T(256)}, f32[256]{0:T(256)S(1)}, u32[]{:S(2)}) copy-start(f32[256]{0:T(256)S(1)} %add_rsqrt_fusion.1) | copy-start | bytes 3076
  8.7 6.6 copy-start.32
  8.7 6.7 copy-start.30
  12.1 153.4 %all-reduce.9.cloned.1.call-start = ((), (), s32[]{:S(2)}) async-start(), calls=%async_computation.10 | async-start | bytes 131072 | tf_op jit(solution)/shard_map/psum | solution.py:162
  112.8 229.5 %reduce-scatter.10.cloned.1.call-start = ((), (), s32[]{:S(2)}) async-start(), calls=%async_computation.11 | async-start | bytes 9437184 | tf_op jit(solution)/shard_map/reduce_scatter | solution.py:185
  271.5 73.7 %copy-start.29 = (f32[1024]{0:T(1024)S(1)}, f32[1024]{0:T(1024)}, u32[]{:S(2)}) copy-start(f32[1024]{0:T(1024)} %param.45) | copy-start | bytes 12292
  271.5 133.3 %all-gather.5.cloned.1.call-start = ((), (), s32[]{:S(2)}) async-start(), calls=%async_computation.12 | async-start | bytes 4718592 | tf_op jit(solution)/shard_map/all_gather | solution.py:212
  342.3 9.4 slice-start
  345.1 19.9 %copy-start.6 = (f32[256,1024]{1,0:T(8,128)}, f32[256,1024]{1,0:T(8,128)S(1)}, u32[]{:S(2)}) copy-start(f32[256,1024]{1,0:T(8,128)S(1)} %get-tuple-element.1028) | copy-start | bytes 3145732
  345.3 6.3 copy-start.10
  345.3 6.3 slice-start.1
  345.4 9.6 slice-start.4
  351.7 3.3 copy-start.15
  351.7 3.3 slice-start.5
  351.7 10.9 slice-start.2
  355.0 7.6 slice-start.3
  362.6 3.7 copy-start.7
  367.9 140.2 %all-reduce.11.cloned.1.call-start = ((), (), s32[]{:S(2)}) async-start(), calls=%async_computation.13 | async-start | bytes 131072 | tf_op jit(solution)/shard_map/psum | solution.py:241
  408.0 2.9 copy-start.23
  455.4 261.9 %reduce-scatter.12.cloned.1.call-start = ((), (), s32[]{:S(2)}) async-start(), calls=%async_computation.14 | async-start | bytes 9437184 | tf_op jit(solution)/shard_map/reduce_scatter | solution.py:299
  508.0 4.2 copy-start.24
  573.8 2.5 copy-start.11
  573.8 2.8 copy-start.21
  586.3 2.5 copy-start.11
  586.4 2.8 copy-start.21
  598.9 2.5 copy-start.11
  598.9 2.8 copy-start.21
  611.5 2.5 copy-start.11
  611.5 2.8 copy-start.21
  646.5 125.5 %reduce-scatter.20.cloned.1.call-start = ((), (), s32[]{:S(2)}) async-start(), calls=%async_computation.18 | async-start | bytes 4718592 | tf_op jit(solution)/shard_map/reduce_scatter | solution.py:317
  651.0 176.2 %reduce-scatter.18.cloned.1.call-start = ((), (), s32[]{:S(2)}) async-start(), calls=%async_computation.17 | async-start | bytes 4718592 | tf_op jit(solution)/shard_map/reduce_scatter | solution.py:316
  655.9 226.0 %reduce-scatter.16.cloned.1.call-start = ((), (), s32[]{:S(2)}) async-start(), calls=%async_computation.16 | async-start | bytes 4718592 | tf_op jit(solution)/shard_map/reduce_scatter | solution.py:315
  661.2 311.2 %reduce-scatter.24.cloned.1.call-start = ((), (), s32[]{:S(2)}) async-start(), calls=%async_computation.20 | async-start | bytes 12976128 | tf_op jit(solution)/shard_map/reduce_scatter | solution.py:320
  669.1 394.0 %reduce-scatter.22.cloned.1.call-start = ((), (), s32[]{:S(2)}) async-start(), calls=%async_computation.19 | async-start | bytes 12976128 | tf_op jit(solution)/shard_map/reduce_scatter | solution.py:319
  676.7 477.0 %reduce-scatter.26.cloned.1.call-start = ((), (), s32[]{:S(2)}) async-start(), calls=%async_computation.21 | async-start | bytes 12976128 | tf_op jit(solution)/shard_map/reduce_scatter | solution.py:321
  684.3 524.4 %reduce-scatter.14.cloned.1.call-start = ((), (), s32[]{:S(2)}) async-start(), calls=%async_computation.15 | async-start | bytes 4718592 | tf_op jit(solution)/shard_map/reduce_scatter | solution.py:314
  721.4 487.3 %copy-start.33 = (u32[32]{0:T(128)S(1)}, u32[32]{0:T(128)}, u32[]{:S(2)}) copy-start(u32[32]{0:T(128)} %constant.261) | copy-start | bytes 388
  721.4 719.5 %all-reduce.13.cloned.1.call-start = ((), (), s32[]{:S(2)}) async-start(), calls=%async_computation.22 | async-start | bytes 12845056 | tf_op jit(solution)/shard_map/psum | solution.py:334
  1210.0 5.9 copy-start.12
  1210.0 5.9 copy-start.13
  1218.4 2.7 copy-start.31
  1440.9 7.8 copy-start.20
  1440.9 8.9 copy-start.19
  1443.0 8.0 copy-start.18
  (21 other events, 39.3 us)
Sparse Core Ops, SparseCore 0:
  12.2 39.4 all-gather.2
  112.9 52.4 all-reduce.8
  271.6 70.6 reduce-scatter.9
  368.0 36.7 all-gather.4
  455.5 52.4 all-reduce.10
  646.7 70.6 reduce-scatter.11
  720.7 51.3 reduce-scatter.19
  775.8 51.3 reduce-scatter.17
  830.5 51.2 reduce-scatter.15
  885.6 86.7 reduce-scatter.23
  976.3 86.7 reduce-scatter.21
  1066.9 86.7 reduce-scatter.25
  1157.4 51.2 reduce-scatter.13
  1211.5 229.3 all-reduce.12
where the time goes:
time: 1470 us; the launch traced here: 1460 us
  waiting for transfers between devices  927 us (63%)
  matrix products  254 us (17%)
  local copies, waits for them, and re-layouts  149 us (10%)
  blocking collectives  49.1 us (3%)
  other arithmetic  39.6 us (3%)
  loops' own time  23.4 us (2%)
  between operations  16.1 us (1%)
    psum x1, waiting for transfers between devices, local(): lax.psum((norm_part, query_part, key_part, value_part, out_part, ffn_gain...  191 us
    reduce_scatter x1, waiting for transfers between devices, local(): lax.psum_scatter(gate_grad, 'mem', scatter_dimension=0, tiled=True)  90.7 us
    reduce_scatter x1, waiting for transfers between devices, local(): lax.psum_scatter(up_grad, 'mem', scatter_dimension=0, tiled=True)  90.6 us
    reduce_scatter x1, waiting for transfers between devices, local(): lax.psum_scatter(down_grad, 'mem', scatter_dimension=0, tiled=True)  90.5 us
    reduce_scatter x1, waiting for transfers between devices, local(): lax.psum_scatter(numerators.reshape(all_rows, model_width), 'mem', scatte...  70.8 us
    reduce_scatter x1, waiting for transfers between devices, local(): lax.psum_scatter(value_grad, 'mem', scatter_dimension=0, tiled=True)  55.1 us
    reduce_scatter x1, waiting for transfers between devices, local(): lax.psum_scatter(query_grad, 'mem', scatter_dimension=0, tiled=True)  55 us
    reduce_scatter x1, waiting for transfers between devices, local(): lax.psum_scatter(key_grad, 'mem', scatter_dimension=0, tiled=True)  54.7 us
  transfers between devices with their start and end apart: 14, of which 14 were waited for; matrix products, arithmetic and copies ran while one was open for 6% of the time, Pallas kernels for 0%

commit v1 on v0

--- a/solution.py
+++ b/solution.py
@@ -159,7 +159,7 @@
     memory_high = lax.dynamic_update_slice_in_dim(memory_high, seg_high, start_block, 0)
     memory_sum = lax.dynamic_update_slice_in_dim(memory_sum, seg_sum, start_block, 0)
     row_high = lax.pmax(memory_high.astype(jnp.bfloat16), "mem").astype(memory_high.dtype)
-    row_sum = lax.psum(memory_sum * jnp.exp(memory_high - row_high), "mem")
+    row_sum = jnp.sum(lax.all_gather(memory_sum * jnp.exp(memory_high - row_high), "mem"), axis=0)
     log_total = row_high + jnp.log(row_sum)
 
     def memory_second(pieces):

time: 1470 us -> 1440 us (0.980)
  waiting for transfers between devices: 927 us -> 878 us
  blocking collectives: 49.1 us -> 72.4 us
    psum x1 -> x0, waiting for transfers between devices: 46.3 us -> none  [local(): row_sum = lax.psum(memory_sum * jnp.exp(memory_high - row_high), 'mem')]
    all_gather x0 -> x1, blocking collectives: none -> 22.8 us  [local(): lax.all_gather(memory_sum * jnp.exp(memory_high - row_high), 'mem')]
    unnamed x85 -> x87, local copies, waits for them, and re-layouts: 35.1 us -> 34.8 us
  transfers between devices with their start and end apart: 14 -> 13, of which waited for: 14 -> 13; matrix products, arithmetic and copies ran while one was open for 6% -> 6% of each run, Pallas kernels for 0% -> 0%
where the time goes in v1:
time: 1440 us; the launch traced here: 1430 us
  waiting for transfers between devices  878 us (61%)
  matrix products  251 us (17%)
  local copies, waits for them, and re-layouts  147 us (10%)
  blocking collectives  72.4 us (5%)
  other arithmetic  39.2 us (3%)
  loops' own time  22.9 us (2%)
  between operations  16.2 us (1%)
    psum x1, waiting for transfers between devices, local(): lax.psum((norm_part, query_part, key_part, value_part, out_part, ffn_gain...  192 us
    reduce_scatter x1, waiting for transfers between devices, local(): lax.psum_scatter(up_grad, 'mem', scatter_dimension=0, tiled=True)  90.3 us
    reduce_scatter x1, waiting for transfers between devices, local(): lax.psum_scatter(down_grad, 'mem', scatter_dimension=0, tiled=True)  90.3 us
    reduce_scatter x1, waiting for transfers between devices, local(): lax.psum_scatter(gate_grad, 'mem', scatter_dimension=0, tiled=True)  90.2 us
    reduce_scatter x1, waiting for transfers between devices, local(): lax.psum_scatter(numerators.reshape(all_rows, model_width), 'mem', scatte...  71.4 us
    reduce_scatter x1, waiting for transfers between devices, local(): lax.psum_scatter(key_grad, 'mem', scatter_dimension=0, tiled=True)  55.1 us
    reduce_scatter x1, waiting for transfers between devices, local(): lax.psum_scatter(value_grad, 'mem', scatter_dimension=0, tiled=True)  54.7 us
    reduce_scatter x1, waiting for transfers between devices, local(): lax.psum_scatter(query_grad, 'mem', scatter_dimension=0, tiled=True)  54.6 us
  transfers between devices with their start and end apart: 13, of which 13 were waited for; matrix products, arithmetic and copies ran while one was open for 6% of the time, Pallas kernels for 0%

profile of v1, /device:TPU:0, one launch (start us, length us, event | category | flops | bytes accessed | tf_op | source)
XLA Modules:
  0.0 1427.7 jit_solution(17964753101726673668)
XLA Ops:
  15.6 22.7 %while.110 = (s32[]{:T(128)}, bf16[4,128,1024]{2,1,0:T(8,128)(2,1)}, bf16[4,128,1024]{2,1,0:T(8,128)(2,1)}, s32[4,128]{1,0:T(4,128)S(1)}, pred[4,128]{1,0:T(4,12...) while((s32[]{:T(128)}, bf16[4,128,1024]{2,1,0:T(8,128)(2,1)}, ...), condition=%wide.region_2.3_spmd.clone, body=%wide.region_1.2_spmd.clone.sunk | while | flops 537657344 | bytes 4721261 | solution.py:114
  43.3 8.3 all-gather.4.cloned.1.call-done
  57.8 20.9 %while.111 = (s32[]{:T(128)}, f32[4,512,8]{1,2,0:T(8,128)S(1)}, f32[4,512,8]{1,2,0:T(8,128)S(1)}, s32[4]{0:T(128)S(1)}, pred[256]{0:T(512)(128)(4,1)S(1)}, /*ind...) while((s32[]{:T(128)}, f32[4,512,8]{1,2,0:T(8,128)S(1)}, ...), condition=%wide.region_10.11_spmd.clone, body=%wide.region_7.10_spmd.clone.sunk | while | flops 277078784 | bytes 10475995 | solution.py:155
  78.7 9.8 while.106
  88.6 23.5 %pmax.7 = bf16[4,512,8]{1,2,0:T(8,128)(2,1)S(1)} all-reduce(bf16[4,512,8]{1,2,0:T(8,128)(2,1)S(1)} %get-tuple-element.1010), channel_id=1, replica_groups=mesh['seg'=4,'mem'=8] {'mem'}, use_global_device_ids=true, to_apply=%region_11.12 | all-reduce | flops 16384 | bytes 65536 | tf_op jit(solution)/shard_map/pmax | solution.py:161
  112.1 22.8 %all-gather = f32[32,512,8]{1,2,0:T(8,128)} all-gather(f32[4,512,8]{1,2,0:T(8,128)S(1)} %fusion.205), channel_id=2, replica_groups=mesh['seg'=4,'mem'=8] {'mem'}, dimensions={0}, use_global_device_ids=true | all-gather | bytes 589824 | tf_op jit(solution)/shard_map/all_gather | solution.py:162
  136.1 4.3 broadcast.311.clone3.1
  140.3 26.2 %while.112 = (s32[]{:T(128)}, f32[4,512,8,128]{3,1,2,0:T(8,128)}, s32[4]{0:T(128)S(1)}, pred[256]{0:T(512)(128)(4,1)S(1)}, s32[]{:T(128)}, /*index=5*/bf16[4,512...) while((s32[]{:T(128)}, f32[4,512,8,128]{3,1,2,0:T(8,128)}, ...), condition=%wide.region_16.17_spmd.clone, body=%wide.region_15.16_spmd.clone.sunk | while | flops 542376704 | bytes 4643303 | solution.py:184
  142.4 4.5 bitcast_dynamic-update-slice_fusion.17
  149.0 4.4 bitcast_dynamic-update-slice_fusion.17
  155.5 4.5 bitcast_dynamic-update-slice_fusion.17
  162.0 4.5 bitcast_dynamic-update-slice_fusion.17
  170.7 46.0 %while.107 = (s32[]{:T(128)}, f32[4,512,8,128]{3,1,2,0:T(8,128)}, bf16[4,128,8,128]{3,2,1,0:T(8,128)(2,1)}, pred[4,128]{1,0:T(4,128)(4,1)S(1)}, bf16[4,128,8,128...) while((s32[]{:T(128)}, f32[4,512,8,128]{3,1,2,0:T(8,128)}, ...), condition=%wide.region_14.15_spmd, body=%wide.region_13.14_spmd.sunk | while | flops 271056896 | bytes 13158765 | solution.py:173
  216.7 10.3 add.248
  227.0 8.2 copy.98
  235.3 5.4 copy.151
  240.7 71.4 %reduce-scatter.10.cloned.1.call-done = f32[256,1024]{1,0:T(8,128)} async-done(((f32[2048,1024]{1,0:T(8,128)}), f32[256,1024]{1,0:T(8,128)}) %reduce-scatter.10.cloned.1.call-update) | async-done | bytes 1048592 | tf_op jit(solution)/shard_map/reduce_scatter | solution.py:185
  315.2 6.3 fusion.216
  324.8 5.9 multiply_convert_fusion
  340.3 34.3 %all-gather.6.cloned.1.call-done = bf16[2048,1024]{1,0:T(8,128)(2,1)} async-done(((bf16[256,1024]{1,0:T(8,128)(2,1)}), bf16[2048,1024]{1,0:T(8,128)(2,1)}) %all-gather.6.cloned.1.call-update) | async-done | bytes 4194320 | tf_op jit(solution)/shard_map/all_gather | solution.py:212
  380.8 28.1 %while.113 = (s32[]{:T(128)}, f32[4,512,8]{1,2,0:T(8,128)S(1)}, s32[4]{0:T(128)S(1)}, pred[256]{0:T(512)(128)(4,1)S(1)}, s32[]{:T(128)}, /*index=5*/bf16[4,512,8...) while((s32[]{:T(128)}, f32[4,512,8]{1,2,0:T(8,128)S(1)}, ...), condition=%wide.region_25.26_spmd.clone, body=%wide.region_23.25_spmd.clone.sunk | while | flops 543421184 | bytes 12032499 | solution.py:240
  408.9 15.7 %while.108 = (s32[]{:T(128)}, f32[4,512,8]{1,2,0:T(8,128)S(1)}, pred[4,128]{1,0:T(4,128)(4,1)S(1)}, bf16[4,128,8,128]{3,1,2,0:T(8,128)(2,1)}, bf16[4,512,8,128]{...) while((s32[]{:T(128)}, f32[4,512,8]{1,2,0:T(8,128)S(1)}, ...), condition=%wide.region_22.23_spmd, body=%wide.region_20.22_spmd.sunk | while | flops 271577088 | bytes 6917489 | solution.py:223
  425.3 52.5 %all-reduce.8.cloned.1.call-done = f32[4,512,8]{1,2,0:T(8,128)} async-done(((f32[4,512,8]{1,2,0:T(8,128)}), f32[4,512,8]{1,2,0:T(8,128)}) %all-reduce.8.cloned.1.call-update) | async-done | bytes 65552 | tf_op jit(solution)/shard_map/psum | solution.py:241
  482.1 55.5 %while.109 = (s32[]{:T(128)}, f32[4,512,8,128]{3,1,2,0:T(8,128)}, bf16[4,128,8,128]{3,1,2,0:T(8,128)(2,1)}, pred[4,128]{1,0:T(4,128)(4,1)S(1)}, bf16[4,512,8,128...) while((s32[]{:T(128)}, f32[4,512,8,128]{3,1,2,0:T(8,128)}, ...), condition=%wide.region_28.29_spmd, body=%wide.region_27.28_spmd.sunk | while | flops 407371776 | bytes 17665912 | solution.py:258
  485.6 4.6 multiply_bitcast_fusion.2
  499.5 4.6 multiply_bitcast_fusion.2
  513.2 4.6 multiply_bitcast_fusion.2
  527.0 4.6 multiply_bitcast_fusion.2
  541.9 50.4 %while.114 = (s32[]{:T(128)}, f32[256,8,128]{0,2,1:T(8,128)}, f32[256,8,128]{0,2,1:T(8,128)}, f32[4,512,8,128]{3,1,2,0:T(8,128)}, s32[4]{0:T(128)S(1)}, /*index=...) while((s32[]{:T(128)}, f32[256,8,128]{0,2,1:T(8,128)}, ...), condition=%wide.region_30.31_spmd.clone, body=%wide.region_29.30_spmd.clone.sunk | while | flops 1357906688 | bytes 65264296 | solution.py:295
  592.3 10.3 add.257
  602.6 8.2 copy.117
  610.9 5.4 copy.150
  616.3 4.4 fusion.199
  631.2 7.6 fusion.219
  638.9 7.5 fusion.218
  646.5 7.6 fusion.220
  654.2 33.0 %reduce-scatter.12.cloned.1.call-done = f32[256,1024]{1,0:T(8,128)} async-done(((f32[2048,1024]{1,0:T(8,128)}), f32[256,1024]{1,0:T(8,128)}) %reduce-scatter.12.cloned.1.call-update) | async-done | bytes 1048592 | tf_op jit(solution)/shard_map/reduce_scatter | solution.py:299
  691.2 50.8 %reduce-scatter.20.cloned.1.call-done = f32[128,1024]{1,0:T(8,128)} async-done(((f32[1024,1024]{1,0:T(8,128)}), f32[128,1024]{1,0:T(8,128)}) %reduce-scatter.20.cloned.1.call-update) | async-done | bytes 524304 | tf_op jit(solution)/shard_map/reduce_scatter | solution.py:317
  742.1 54.7 %reduce-scatter.18.cloned.1.call-done = f32[128,1024]{1,0:T(8,128)} async-done(((f32[1024,1024]{1,0:T(8,128)}), f32[128,1024]{1,0:T(8,128)}) %reduce-scatter.18.cloned.1.call-update) | async-done | bytes 524304 | tf_op jit(solution)/shard_map/reduce_scatter | solution.py:316
  796.7 55.1 %reduce-scatter.16.cloned.1.call-done = f32[128,1024]{1,0:T(8,128)} async-done(((f32[1024,1024]{1,0:T(8,128)}), f32[128,1024]{1,0:T(8,128)}) %reduce-scatter.16.cloned.1.call-update) | async-done | bytes 524304 | tf_op jit(solution)/shard_map/reduce_scatter | solution.py:315
  851.9 90.3 %reduce-scatter.24.cloned.1.call-done = f32[128,2816]{1,0:T(8,128)} async-done(((f32[1024,2816]{1,0:T(8,128)}), f32[128,2816]{1,0:T(8,128)}) %reduce-scatter.24.cloned.1.call-update) | async-done | bytes 1441808 | tf_op jit(solution)/shard_map/reduce_scatter | solution.py:320
  942.2 90.2 %reduce-scatter.22.cloned.1.call-done = f32[128,2816]{1,0:T(8,128)} async-done(((f32[1024,2816]{1,0:T(8,128)}), f32[128,2816]{1,0:T(8,128)}) %reduce-scatter.22.cloned.1.call-update) | async-done | bytes 1441808 | tf_op jit(solution)/shard_map/reduce_scatter | solution.py:319
  1032.4 90.3 %reduce-scatter.26.cloned.1.call-done = f32[352,1024]{1,0:T(8,128)} async-done(((f32[2816,1024]{1,0:T(8,128)}), f32[352,1024]{1,0:T(8,128)}) %reduce-scatter.26.cloned.1.call-update) | async-done | bytes 1441808 | tf_op jit(solution)/shard_map/reduce_scatter | solution.py:321
  1122.7 54.6 %reduce-scatter.14.cloned.1.call-done = f32[128,1024]{1,0:T(8,128)} async-done(((f32[1024,1024]{1,0:T(8,128)}), f32[128,1024]{1,0:T(8,128)}) %reduce-scatter.14.cloned.1.call-update) | async-done | bytes 524304 | tf_op jit(solution)/shard_map/reduce_scatter | solution.py:314
  1178.5 5.9 fusion.184
  1189.2 13.5 all-reduce.2
  1202.9 12.5 all-reduce.3
  1218.0 191.8 %all-reduce.10.cloned.1.call-done = (f32[128,1024]{1,0:T(8,128)}, f32[128,1024]{1,0:T(8,128)}, f32[128,1024]{1,0:T(8,128)}, f32[128,1024]{1,0:T(8,128)}, f32[128...) async-done(((f32[128,1024]{1,0:T(8,128)}, f32[128,1024]{1,0:T(8,128)}, f32[128,1024]{1,0:T(8,128)}, f32[128,1024]{1,0:T(8,128)}, f32[128,2816]{1,0:T(8,128)}, ...) | async-done | bytes 6422544 | tf_op jit(solution)/shard_map/psum | solution.py:334
  (430 shorter events, 305.1 us)
Async XLA Ops:
  7.2 5.8 copy-start
  7.2 5.7 copy-start.3
  7.2 5.7 copy-start.26
  7.2 44.4 %all-gather.4.cloned.1.call-start = ((), (), s32[]{:S(2)}) async-start(), calls=%async_computation.9 | async-start | bytes 4718592 | tf_op jit(solution)/shard_map/all_gather | solution.py:115
  8.6 6.0 copy-start.28
  12.0 300.1 %reduce-scatter.10.cloned.1.call-start = ((), (), s32[]{:S(2)}) async-start(), calls=%async_computation.10 | async-start | bytes 9437184 | tf_op jit(solution)/shard_map/reduce_scatter | solution.py:185
  12.1 2.5 copy-start.14
  13.0 2.6 copy-start.31
  15.6 25.2 %copy-start.33 = (s32[256]{0:T(256)S(1)}, s32[256]{0:T(256)}, u32[]{:S(2)}) copy-start(s32[256]{0:T(256)} %param.35) | copy-start | bytes 3076
  240.6 74.4 %copy-start.30 = (f32[1024]{0:T(1024)S(1)}, f32[1024]{0:T(1024)}, u32[]{:S(2)}) copy-start(f32[1024]{0:T(1024)} %param.45) | copy-start | bytes 12292
  240.7 133.9 %all-gather.6.cloned.1.call-start = ((), (), s32[]{:S(2)}) async-start(), calls=%async_computation.11 | async-start | bytes 4718592 | tf_op jit(solution)/shard_map/all_gather | solution.py:212
  312.1 9.4 slice-start
  315.0 19.9 %copy-start.6 = (f32[256,1024]{1,0:T(8,128)}, f32[256,1024]{1,0:T(8,128)S(1)}, u32[]{:S(2)}) copy-start(f32[256,1024]{1,0:T(8,128)S(1)} %get-tuple-element.1028) | copy-start | bytes 3145732
  315.2 6.3 copy-start.10
  315.2 6.3 slice-start.1
  315.2 9.6 slice-start.4
  321.5 3.3 copy-start.16
  321.5 3.3 slice-start.5
  321.5 10.9 slice-start.2
  324.8 7.7 slice-start.3
  332.5 3.7 copy-start.7
  337.8 140.1 %all-reduce.8.cloned.1.call-start = ((), (), s32[]{:S(2)}) async-start(), calls=%async_computation.12 | async-start | bytes 131072 | tf_op jit(solution)/shard_map/psum | solution.py:241
  377.9 2.9 copy-start.24
  425.3 261.8 %reduce-scatter.12.cloned.1.call-start = ((), (), s32[]{:S(2)}) async-start(), calls=%async_computation.13 | async-start | bytes 9437184 | tf_op jit(solution)/shard_map/reduce_scatter | solution.py:299
  477.9 4.2 copy-start.25
  543.8 2.5 copy-start.11
  543.8 2.8 copy-start.22
  556.3 2.5 copy-start.11
  556.3 2.8 copy-start.22
  568.8 2.5 copy-start.11
  568.8 2.8 copy-start.22
  581.4 2.5 copy-start.11
  581.4 2.8 copy-start.22
  616.3 125.8 %reduce-scatter.20.cloned.1.call-start = ((), (), s32[]{:S(2)}) async-start(), calls=%async_computation.17 | async-start | bytes 4718592 | tf_op jit(solution)/shard_map/reduce_scatter | solution.py:317
  620.7 176.0 %reduce-scatter.18.cloned.1.call-start = ((), (), s32[]{:S(2)}) async-start(), calls=%async_computation.16 | async-start | bytes 4718592 | tf_op jit(solution)/shard_map/reduce_scatter | solution.py:316
  625.6 226.2 %reduce-scatter.16.cloned.1.call-start = ((), (), s32[]{:S(2)}) async-start(), calls=%async_computation.15 | async-start | bytes 4718592 | tf_op jit(solution)/shard_map/reduce_scatter | solution.py:315
  631.0 311.2 %reduce-scatter.24.cloned.1.call-start = ((), (), s32[]{:S(2)}) async-start(), calls=%async_computation.19 | async-start | bytes 12976128 | tf_op jit(solution)/shard_map/reduce_scatter | solution.py:320
  638.9 393.5 %reduce-scatter.22.cloned.1.call-start = ((), (), s32[]{:S(2)}) async-start(), calls=%async_computation.18 | async-start | bytes 12976128 | tf_op jit(solution)/shard_map/reduce_scatter | solution.py:319
  646.4 476.3 %reduce-scatter.26.cloned.1.call-start = ((), (), s32[]{:S(2)}) async-start(), calls=%async_computation.20 | async-start | bytes 12976128 | tf_op jit(solution)/shard_map/reduce_scatter | solution.py:321
  654.1 523.1 %reduce-scatter.14.cloned.1.call-start = ((), (), s32[]{:S(2)}) async-start(), calls=%async_computation.14 | async-start | bytes 4718592 | tf_op jit(solution)/shard_map/reduce_scatter | solution.py:314
  691.2 486.1 %copy-start.34 = (u32[32]{0:T(128)S(1)}, u32[32]{0:T(128)}, u32[]{:S(2)}) copy-start(u32[32]{0:T(128)} %constant.261) | copy-start | bytes 388
  691.2 718.7 %all-reduce.10.cloned.1.call-start = ((), (), s32[]{:S(2)}) async-start(), calls=%async_computation.21 | async-start | bytes 12845056 | tf_op jit(solution)/shard_map/psum | solution.py:334
  1178.5 5.9 copy-start.12
  1178.5 5.9 copy-start.13
  1186.5 2.7 copy-start.32
  1409.9 7.8 copy-start.21
  1409.9 8.9 copy-start.20
  1411.9 8.0 copy-start.19
  (21 other events, 38.8 us)
Sparse Core Ops, SparseCore 0:
  12.1 39.4 all-gather.3
  240.8 71.2 reduce-scatter.9
  337.9 36.6 all-gather.5
  425.4 52.4 all-reduce.7
  616.4 70.6 reduce-scatter.11
  690.7 51.3 reduce-scatter.19
  745.4 51.2 reduce-scatter.17
  800.5 51.3 reduce-scatter.15
  855.4 86.7 reduce-scatter.23
  945.5 86.7 reduce-scatter.21
  1035.9 86.7 reduce-scatter.25
  1125.9 51.3 reduce-scatter.13
  1180.5 229.3 all-reduce.9
